TPU v7x, 32 devices: a whole 2x2x4 slice. The times are simulated.
32 devices in a mesh: fsdp: 8 (over y, x, core), ctx: 4 (over z).
Axes of the slice: x: 2, y: 2, z: 4, core: 2. Of those that a mesh axis runs over, the one named last changes fastest.
Arguments:
- inputs: bfloat16 [8, 4096, 1024], P('fsdp', 'ctx'), may hold values from -6 to 6
- cotangent: bfloat16 [8, 4096, 1024], P('fsdp', 'ctx'), may hold values from -6 to 6
- positions: int32 [8, 4096], P('fsdp', 'ctx'), may hold values from 0 to 2303, as said below
- segments: int32 [8, 4096], P('fsdp', 'ctx'), may hold values from 0 to 8, as said below
- ln1_gain: bfloat16 [1024], P('fsdp'), may hold values from 0.5 to 1.5
- ln1_bias: bfloat16 [1024], P('fsdp'), may hold values from -2.5 to 2.5
- w_qkv: bfloat16 [1024, 3072], P('fsdp'), may hold values from -0.1875 to 0.1875
- b_qkv: bfloat16 [3072], P('fsdp'), may hold values from -3 to 3
- w_attn_out: bfloat16 [1024, 1024], P('fsdp'), may hold values from -1.5 to 1.5
- b_out: bfloat16 [1024], P('fsdp'), may hold values from -2.5 to 2.5
- ln2_gain: bfloat16 [1024], P('fsdp'), may hold values from 0.5 to 1.5
- ln2_bias: bfloat16 [1024], P('fsdp'), may hold values from -2.5 to 2.5
- w_in: bfloat16 [1024, 4096], P('fsdp'), may hold values from -0.1875 to 0.1875
- b_in: bfloat16 [4096], P('fsdp'), may hold values from -2.5 to 2.5
- w_out: bfloat16 [4096, 1024], P('fsdp'), may hold values from -0.09375 to 0.09375
Outputs:
- output: bfloat16 [8, 4096, 1024], P('fsdp', 'ctx')
- grad_inputs: float32 [8, 4096, 1024], P('fsdp', 'ctx')
- grad_ln1_gain: float32 [1024], P(('fsdp', 'ctx'))
- grad_ln1_bias: float32 [1024], P(('fsdp', 'ctx'))
- grad_w_qkv: float32 [1024, 3072], P(('fsdp', 'ctx'))
- grad_b_qkv: float32 [3072], P(('fsdp', 'ctx'))
- grad_w_attn_out: float32 [1024, 1024], P(('fsdp', 'ctx'))
- grad_b_out: float32 [1024], P(('fsdp', 'ctx'))
- grad_ln2_gain: float32 [1024], P(('fsdp', 'ctx'))
- grad_ln2_bias: float32 [1024], P(('fsdp', 'ctx'))
- grad_w_in: float32 [1024, 4096], P(('fsdp', 'ctx'))
- grad_b_in: float32 [4096], P(('fsdp', 'ctx'))
- grad_w_out: float32 [4096, 1024], P(('fsdp', 'ctx'))
Inputs may be any that keep to these rules, and one draw needn't show every extreme that they name: `positions`: in a group, token t of the natural order (the prompt, then the continuations one after another) has position t and segment 0 if t < 2048, else position 2048 + (t - 2048) % 256 and segment 1 + (t - 2048) // 256. The natural order is cut into 8 blocks of 512 tokens; index j of ctx holds block p_j followed by block 7 - p_j, where p is a permutation of 0 to 3 drawn for each group. `segments`: laid out with positions as stated there.
All inputs are finite; a program needn't handle non-finite values.
Results may differ from a plain program's by a relative error of at most 0.014.
Values may be sent and summed in bfloat16 or wider, within the bound.
No kernel may reach another device: no remote copies, remote signals or barrier semaphores. Data moves between devices by JAX's collectives and lax.ppermute only.
A program may use at most 256 MiB of HBM per device.

v0:
```python
from functools import partial
import math
import jax
import jax.numpy as jnp
from jax import lax
from jax.sharding import PartitionSpec as P

HEADS = 16
HD = 64
ROT = 16
NORM_EPS = 1e-05
MASKED = -1e30


def layer_norm(values, scaling, offset):
    average = jnp.mean(values, axis=-1, keepdims=True)
    centered = values - average
    variance = jnp.mean(centered * centered, axis=-1, keepdims=True)
    return centered * lax.rsqrt(variance + NORM_EPS) * scaling + offset


def rotary_tables(positions):
    halfway = ROT // 2
    spacing = jnp.arange(halfway, dtype=jnp.float32) * (2.0 / ROT)
    inverse = jnp.exp(-math.log(10000.0) * spacing)
    angles = positions.astype(jnp.float32)[..., None] * inverse
    return (jnp.cos(angles), jnp.sin(angles))


def rotate(heads_in, cosine, sine):
    halfway = ROT // 2
    cosine = cosine[..., None, :]
    sine = sine[..., None, :]
    first = heads_in[..., :halfway]
    second = heads_in[..., halfway:ROT]
    return jnp.concatenate(
        [first * cosine - second * sine, second * cosine + first * sine, heads_in[..., ROT:]],
        axis=-1,
    )


def unrotate(grads_in, cosine, sine):
    halfway = ROT // 2
    cosine = cosine[..., None, :]
    sine = sine[..., None, :]
    first = grads_in[..., :halfway]
    second = grads_in[..., halfway:ROT]
    return jnp.concatenate(
        [first * cosine + second * sine, second * cosine - first * sine, grads_in[..., ROT:]],
        axis=-1,
    )


def allowed_mask(query_pos, query_seg, key_pos, key_seg):
    same_doc = (key_seg[:, None, :] == 0) | (key_seg[:, None, :] == query_seg[:, :, None])
    causal = key_pos[:, None, :] <= query_pos[:, :, None]
    return (same_doc & causal)[:, None]


def scores_of(queries, keys_blk):
    return jnp.einsum("gqhd,gkhd->ghqk", queries, keys_blk, preferred_element_type=jnp.float32)


def block_grads(queries, grad_att, log_total, delta, mask, keys_blk, values_blk):
    probs = jnp.where(mask, jnp.exp(scores_of(queries, keys_blk) - log_total[..., None]), 0.0)
    dprobs = jnp.einsum("gqhd,gkhd->ghqk", grad_att, values_blk, preferred_element_type=jnp.float32)
    grad_scores = (probs * (dprobs - delta[..., None])).astype(jnp.bfloat16)
    return (probs.astype(jnp.bfloat16), grad_scores)


def local(
    inputs,
    cotangent,
    positions,
    segments,
    ln1_gain,
    ln1_bias,
    w_qkv,
    b_qkv,
    w_attn_out,
    b_out,
    ln2_gain,
    ln2_bias,
    w_in,
    b_in,
    w_out,
):
    shards = (
        ln1_gain,
        ln1_bias,
        w_qkv,
        b_qkv,
        w_attn_out,
        b_out,
        ln2_gain,
        ln2_bias,
        w_in,
        b_in,
        w_out,
    )
    params = (
        lax.all_gather(shards[0], "fsdp", axis=0, tiled=True),
        lax.all_gather(shards[1], "fsdp", axis=0, tiled=True),
        lax.all_gather(shards[2], "fsdp", axis=0, tiled=True),
        lax.all_gather(shards[3], "fsdp", axis=0, tiled=True),
        lax.all_gather(shards[4], "fsdp", axis=0, tiled=True),
        lax.all_gather(shards[5], "fsdp", axis=0, tiled=True),
        lax.all_gather(shards[6], "fsdp", axis=0, tiled=True),
        lax.all_gather(shards[7], "fsdp", axis=0, tiled=True),
        lax.all_gather(shards[8], "fsdp", axis=0, tiled=True),
        lax.all_gather(shards[9], "fsdp", axis=0, tiled=True),
        lax.all_gather(shards[10], "fsdp", axis=0, tiled=True),
    )
    groups, local_len, width = inputs.shape
    rows_total = groups * local_len
    block = math.gcd(local_len, 256)
    label_pos, label_seg = (
        lax.all_gather(positions, "ctx", axis=1, tiled=True),
        lax.all_gather(segments, "ctx", axis=1, tiled=True),
    )
    count = label_pos.shape[1] // block
    f32 = jnp.float32
    bf16 = jnp.bfloat16
    (
        gain_attn,
        shift_attn,
        weight_qkv,
        bias_qkv,
        weight_attn,
        bias_out,
        gain_mlp,
        shift_mlp,
        weight_in,
        bias_in,
        weight_out,
    ) = params
    flat_in = inputs.reshape(rows_total, width).astype(f32)
    normed_attn = layer_norm(flat_in, gain_attn.astype(f32), shift_attn.astype(f32)).astype(bf16)
    normed_mlp = layer_norm(flat_in, gain_mlp.astype(f32), shift_mlp.astype(f32)).astype(bf16)
    projected = jnp.dot(normed_attn, weight_qkv, preferred_element_type=f32) + bias_qkv.astype(f32)
    cosine, sine = rotary_tables(positions)

    def split_heads(columns):
        return columns.reshape(groups, local_len, HEADS, HD)

    scale = HD ** (-0.5)
    queries = (rotate(split_heads(projected[:, :width]), cosine, sine) * scale).astype(bf16)
    keys_own = rotate(split_heads(projected[:, width : 2 * width]), cosine, sine).astype(bf16)
    values_own = split_heads(projected[:, 2 * width :]).astype(bf16)
    keys_all, values_all = (
        lax.all_gather(keys_own, "ctx", axis=1, tiled=True),
        lax.all_gather(values_own, "ctx", axis=1, tiled=True),
    )

    def key_block(index):
        start = index * block
        keys_blk = lax.dynamic_slice_in_dim(keys_all, start, block, 1)
        values_blk = lax.dynamic_slice_in_dim(values_all, start, block, 1)
        mask = allowed_mask(
            positions,
            segments,
            lax.dynamic_slice_in_dim(label_pos, start, block, 1),
            lax.dynamic_slice_in_dim(label_seg, start, block, 1),
        )
        return (keys_blk, values_blk, mask)

    def total_step(carry, index):
        peak, total = carry
        keys_blk, values_blk, mask = key_block(index)
        scores = jnp.where(mask, scores_of(queries, keys_blk), MASKED)
        fresh = jnp.maximum(peak, jnp.max(scores, axis=-1))
        added = jnp.sum(jnp.where(mask, jnp.exp(scores - fresh[..., None]), 0.0), axis=-1)
        return ((fresh, total * jnp.exp(peak - fresh) + added), None)

    stat_shape = (groups, HEADS, local_len)
    (peak, total), unused = lax.scan(
        total_step,
        (jnp.full(stat_shape, MASKED, f32), jnp.zeros(stat_shape, f32)),
        jnp.arange(count),
    )
    log_total = peak + jnp.log(total)

    def attend_step(rounded_sum, index):
        keys_blk, values_blk, mask = key_block(index)
        probs = jnp.where(mask, jnp.exp(scores_of(queries, keys_blk) - log_total[..., None]), 0.0)
        rounded_sum = rounded_sum + jnp.einsum(
            "ghqk,gkhd->gqhd", probs.astype(bf16), values_blk, preferred_element_type=f32
        )
        return (rounded_sum, None)

    head_shape = (groups, local_len, HEADS, HD)
    rounded_sum, unused = lax.scan(attend_step, jnp.zeros(head_shape, f32), jnp.arange(count))
    attended = rounded_sum.reshape(rows_total, width).astype(bf16)
    pre_act = jnp.dot(normed_mlp, weight_in, preferred_element_type=f32) + bias_in.astype(f32)
    activated = jax.nn.gelu(pre_act, approximate=False).astype(bf16)
    output = (
        flat_in
        + jnp.dot(attended, weight_attn, preferred_element_type=f32)
        + jnp.dot(activated, weight_out, preferred_element_type=f32)
        + bias_out.astype(f32)
    )
    (
        gain_attn,
        shift_attn,
        weight_qkv,
        bias_qkv,
        weight_attn,
        bias_out,
        gain_mlp,
        shift_mlp,
        weight_in,
        bias_in,
        weight_out,
    ) = params
    grad_out = cotangent.reshape(rows_total, width)
    grad_bias_out = jnp.sum(grad_out.astype(f32), axis=0)
    grad_weight_out = jnp.einsum("rf,rd->fd", activated, grad_out, preferred_element_type=f32)
    grad_act = jnp.einsum("rd,fd->rf", grad_out, weight_out, preferred_element_type=f32)
    unused, gelu_back = jax.vjp(partial(jax.nn.gelu, approximate=False), pre_act)
    grad_pre = gelu_back(grad_act)[0].astype(bf16)
    grad_weight_in = jnp.einsum("rd,rf->df", normed_mlp, grad_pre, preferred_element_type=f32)
    grad_bias_in = jnp.sum(grad_pre.astype(f32), axis=0)
    grad_normed_mlp = jnp.einsum("rf,df->rd", grad_pre, weight_in, preferred_element_type=f32)
    grad_weight_attn = jnp.einsum("ra,rd->ad", attended, grad_out, preferred_element_type=f32)
    grad_att = (
        jnp.einsum("rd,ad->ra", grad_out, weight_attn, preferred_element_type=f32)
        .astype(bf16)
        .reshape(head_shape)
    )
    delta = jnp.einsum(
        "gqhd,gqhd->ghq", grad_att.astype(f32), rounded_sum, precision=lax.Precision.HIGHEST
    )

    def back_step(carry, index):
        keys_blk, values_blk, mask = key_block(index)
        rounded, grad_scores = block_grads(
            queries, grad_att, log_total, delta, mask, keys_blk, values_blk
        )
        carry = carry + jnp.einsum(
            "ghqk,gkhd->gqhd", grad_scores, keys_blk, preferred_element_type=f32
        )
        key_term = jnp.einsum("ghqk,gqhd->gkhd", grad_scores, queries, preferred_element_type=f32)
        value_term = jnp.einsum("ghqk,gqhd->gkhd", rounded, grad_att, preferred_element_type=f32)
        return (carry, (key_term, value_term))

    grad_queries, (key_terms, value_terms) = lax.scan(
        back_step, jnp.zeros(head_shape, f32), jnp.arange(count)
    )
    key_sums, value_sums = (
        lax.psum_scatter(
            key_terms.astype(jnp.bfloat16), "ctx", scatter_dimension=0, tiled=True
        ).astype(jnp.float32),
        lax.psum_scatter(
            value_terms.astype(jnp.bfloat16), "ctx", scatter_dimension=0, tiled=True
        ).astype(jnp.float32),
    )
    grad_keys = jnp.transpose(key_sums, (1, 0, 2, 3, 4)).reshape(head_shape)
    grad_values = jnp.transpose(value_sums, (1, 0, 2, 3, 4)).reshape(head_shape)
    grad_q_pre = unrotate(grad_queries * scale, cosine, sine).reshape(rows_total, width)
    grad_k_pre = unrotate(grad_keys, cosine, sine).reshape(rows_total, width)
    grad_projected = jnp.concatenate(
        [grad_q_pre, grad_k_pre, grad_values.reshape(rows_total, width)], axis=1
    ).astype(bf16)
    grad_weight_qkv = jnp.einsum(
        "rd,re->de", normed_attn, grad_projected, preferred_element_type=f32
    )
    grad_bias_qkv = jnp.sum(grad_projected.astype(f32), axis=0)
    grad_normed_attn = jnp.einsum(
        "re,de->rd", grad_projected, weight_qkv, preferred_element_type=f32
    )
    unused, norm_back_attn = jax.vjp(
        layer_norm, flat_in, gain_attn.astype(f32), shift_attn.astype(f32)
    )
    grad_in_attn, grad_gain_attn, grad_shift_attn = norm_back_attn(grad_normed_attn)
    unused, norm_back_mlp = jax.vjp(
        layer_norm, flat_in, gain_mlp.astype(f32), shift_mlp.astype(f32)
    )
    grad_in_mlp, grad_gain_mlp, grad_shift_mlp = norm_back_mlp(grad_normed_mlp)
    grad_inputs = (grad_out.astype(f32) + grad_in_attn + grad_in_mlp).reshape(
        groups, local_len, width
    )
    sums = (
        lax.psum_scatter(grad_gain_attn, ("fsdp", "ctx"), scatter_dimension=0, tiled=True),
        lax.psum_scatter(grad_shift_attn, ("fsdp", "ctx"), scatter_dimension=0, tiled=True),
        lax.psum_scatter(grad_weight_qkv, ("fsdp", "ctx"), scatter_dimension=0, tiled=True),
        lax.psum_scatter(grad_bias_qkv, ("fsdp", "ctx"), scatter_dimension=0, tiled=True),
        lax.psum_scatter(grad_weight_attn, ("fsdp", "ctx"), scatter_dimension=0, tiled=True),
        lax.psum_scatter(grad_bias_out, ("fsdp", "ctx"), scatter_dimension=0, tiled=True),
        lax.psum_scatter(grad_gain_mlp, ("fsdp", "ctx"), scatter_dimension=0, tiled=True),
        lax.psum_scatter(grad_shift_mlp, ("fsdp", "ctx"), scatter_dimension=0, tiled=True),
        lax.psum_scatter(grad_weight_in, ("fsdp", "ctx"), scatter_dimension=0, tiled=True),
        lax.psum_scatter(grad_bias_in, ("fsdp", "ctx"), scatter_dimension=0, tiled=True),
        lax.psum_scatter(grad_weight_out, ("fsdp", "ctx"), scatter_dimension=0, tiled=True),
    )
    result = output.reshape(groups, local_len, width).astype(bf16)
    return (
        result,
        grad_inputs,
        sums[0],
        sums[1],
        sums[2],
        sums[3],
        sums[4],
        sums[5],
        sums[6],
        sums[7],
        sums[8],
        sums[9],
        sums[10],
    )


def solution(mesh):
    in_specs = (
        P("fsdp", "ctx", None),
        P("fsdp", "ctx", None),
        P("fsdp", "ctx"),
        P("fsdp", "ctx"),
        P("fsdp"),
        P("fsdp"),
        P("fsdp", None),
        P("fsdp"),
        P("fsdp", None),
        P("fsdp"),
        P("fsdp"),
        P("fsdp"),
        P("fsdp", None),
        P("fsdp"),
        P("fsdp", None),
    )
    out_specs = (
        P("fsdp", "ctx", None),
        P("fsdp", "ctx", None),
        P(("fsdp", "ctx")),
        P(("fsdp", "ctx")),
        P(("fsdp", "ctx"), None),
        P(("fsdp", "ctx")),
        P(("fsdp", "ctx"), None),
        P(("fsdp", "ctx")),
        P(("fsdp", "ctx")),
        P(("fsdp", "ctx")),
        P(("fsdp", "ctx"), None),
        P(("fsdp", "ctx")),
        P(("fsdp", "ctx"), None),
    )
    return jax.shard_map(local, mesh=mesh, in_specs=in_specs, out_specs=out_specs, check_vma=False)
```

profile of v0, /device:TPU:0, one launch (start us, length us, event | category | flops | bytes accessed | tf_op | source)
XLA Modules:
  0.0 2799.0 jit_solution(5648398646766879114)
XLA Ops:
  8.0 10.3 all-gather
  40.2 18.0 all-gather.14.cloned.1.call-done
  98.3 13.3 all_gather.51
  111.5 18.1 all_gather.50
  133.6 107.9 %all-gather.18.cloned.1.call-done = bf16[1,4096,16,64]{1,3,2,0:T(8,128)(2,1)} async-done(((bf16[1,1024,16,64]{1,3,2,0:T(8,128)(2,1)}), bf16[1,4096,16,64]{1,3,2,0:T(8,128)(2,1)}) %all-gather.18.cloned.1.call-update) | async-done | bytes 8388624 | tf_op jit(solution)/shard_map/all_gather | solution.py:151
  241.4 326.4 %while.39 = (s32[]{:T(128)}, f32[1,16,1024]{2,1,0:T(8,128)S(1)}, f32[1,16,1024]{2,1,0:T(8,128)S(1)}, s32[16]{0:T(128)S(1)}, s32[1,4096]{1,0:T(1,128)S(1)}, /*ind...) while((s32[]{:T(128)}, f32[1,16,1024]{2,1,0:T(8,128)S(1)}, ...), condition=%wide.region_5.6_spmd.clone, body=%wide.region_2.5_spmd.clone.sunk | while | flops 563167488 | bytes 37830352 | solution.py:176
  243.1 11.0 fusion.159
  567.9 167.2 %while.40 = (s32[]{:T(128)}, f32[1,1024,16,64]{1,3,2,0:T(8,128)}, s32[16]{0:T(128)S(1)}, bf16[1,4096,16,64]{1,3,2,0:T(8,128)(2,1)}, s32[1,4096]{1,0:T(1,128)S(1)...) while((s32[]{:T(128)}, f32[1,1024,16,64]{1,3,2,0:T(8,128)}, ...), condition=%wide.region_7.8_spmd.clone, body=%wide.region_6.7_spmd.clone.sunk | while | flops 1089470720 | bytes 12141780 | solution.py:192
  742.4 715.6 %while.41 = (s32[]{:T(128)}, f32[1,1024,16,64]{1,3,2,0:T(8,128)}, bf16[16,1,256,16,64]{2,4,3,1,0:T(8,128)(2,1)}, bf16[16,1,256,16,64]{2,4,3,1,0:T(8,128)(2,1)}, ...) while((s32[]{:T(128)}, f32[1,1024,16,64]{1,3,2,0:T(8,128)}, ...), condition=%wide.region_9.10_spmd.clone, body=%wide.region_8.9_spmd.clone.sunk | while | flops 2721054976 | bytes 138887984 | solution.py:246
  776.0 10.0 fusion.176
  865.7 9.9 fusion.176
  910.5 9.9 fusion.176
  955.3 9.9 fusion.176
  1134.5 9.9 fusion.176
  1179.3 9.9 fusion.176
  1224.1 9.9 fusion.176
  1268.9 9.9 fusion.176
  1313.7 9.9 fusion.176
  1494.4 50.9 %multiply_convert_fusion = (bf16[1024,4096]{1,0:T(8,128)(2,1)}, f32[1024,4096]{1,0:T(8,128)}, f32[1024,4096]{1,0:T(8,128)}) fusion(f32[4096]{0:T(1024)S(1)} %bitcast.419, bf16[1024,4096]{1,0:T(8,128)(2,1)} %all-gather.22.cloned.1.call-done, bf16[1,1024,1024]{2,1,0:T(8,128)(2,1)S(1)} %copy-done.3, f32[1024]{0:T(1024)S(1)} %bitcast.424, ...), kind=kOutput, calls=%fused_computation.67 | convolution fusion | flops 8873050112 | bytes 52461568 | tf_op jit(solution)/shard_map/dot_general | solution.py:194
  1545.3 24.3 convert_reduce_fusion
  1569.6 15.1 fusion.109
  1584.7 16.6 fusion.95
  1613.3 136.2 %reduce-scatter.9.cloned.1.call-done = bf16[4,1,256,16,64]{2,4,3,1,0:T(8,128)(2,1)} async-done(((bf16[16,1,256,16,64]{2,4,3,1,0:T(8,128)(2,1)}), bf16[4,1,256,16,64]{2,4,3,1,0:T(8,128)(2,1)}) %reduce-scatter.9.cloned.1.call-update) | async-done | bytes 2097168 | tf_op jit(solution)/shard_map/reduce_scatter | solution.py:253
  1759.0 11.7 fusion.113
  1780.0 13.1 fusion.124
  1795.5 14.9 fusion.94
  1810.4 13.5 fusion.120
  1838.5 41.4 %all-reduce.7 = (f32[1024]{0:T(1024)S(1)}, f32[1024]{0:T(1024)S(1)}, f32[3072]{0:T(1024)S(1)}, f32[1024]{0:T(1024)S(1)}, f32[1024]{0:T(1024)S(1)}, /*index=5*/f32[1024]{0:T(1024)S(1)}, f32[4096]{0:T(1024)S(1)}) all-reduce(f32[1024]{0:T(1024)S(1)} %get-tuple-element.356, ...), channel_id=4, replica_groups=mesh['fsdp'=8,'ctx'=4] {'fsdp','ctx'}, use_global_device_ids=true, to_apply=%region_17.18.clone | all-reduce | flops 12288 | bytes 98304
  1884.0 17.0 reduce-scatter.13.cloned.1.call-done
  1901.0 366.0 %reduce-scatter.15.cloned.1.call-done = f32[32,4096]{1,0:T(8,128)} async-done(((f32[1024,4096]{1,0:T(8,128)}), f32[32,4096]{1,0:T(8,128)}) %reduce-scatter.15.cloned.1.call-update) | async-done | bytes 524304 | tf_op jit(solution)/shard_map/reduce_scatter | solution.py:291
  2267.0 365.1 %reduce-scatter.17.cloned.1.call-done = f32[128,1024]{1,0:T(8,128)} async-done(((f32[4096,1024]{1,0:T(8,128)}), f32[128,1024]{1,0:T(8,128)}) %reduce-scatter.17.cloned.1.call-update) | async-done | bytes 524304 | tf_op jit(solution)/shard_map/reduce_scatter | solution.py:293
  2632.0 159.8 %reduce-scatter.11.cloned.1.call-done = f32[32,3072]{1,0:T(8,128)} async-done(((f32[1024,3072]{1,0:T(8,128)}), f32[32,3072]{1,0:T(8,128)}) %reduce-scatter.11.cloned.1.call-update) | async-done | bytes 393232 | tf_op jit(solution)/shard_map/reduce_scatter | solution.py:285
  (596 shorter events, 1236.7 us)
Async XLA Ops:
  7.2 31.5 %copy-start.2 = (bf16[1,1024,1024]{2,1,0:T(8,128)(2,1)S(1)}, bf16[1,1024,1024]{2,1,0:T(8,128)(2,1)}, u32[]{:S(2)}) copy-start(bf16[1,1024,1024]{2,1,0:T(8,128)(2,1)} %param.21) | copy-start | bytes 6291460
  7.2 51.0 %all-gather.14.cloned.1.call-start = ((), (), s32[]{:S(2)}) async-start(), calls=%async_computation.6 | async-start | bytes 7077888 | tf_op jit(solution)/shard_map/all_gather | solution.py:104
  7.9 233.5 %all-gather.18.cloned.1.call-start = ((), (), s32[]{:S(2)}) async-start(), calls=%async_computation.8 | async-start | bytes 10485760 | tf_op jit(solution)/shard_map/all_gather | solution.py:151
  18.3 48.9 %copy-start.27 = (f32[8,1,128]{2,1,0:T(1,128)}, f32[8,1,128]{2,1,0:T(1,128)S(1)}, u32[]{:S(2)}) copy-start(f32[8,1,128]{2,1,0:T(1,128)S(1)} %convert_element_type.150) | copy-start | bytes 12292
  26.9 40.3 %copy-start.33 = (f32[8,1,128]{2,1,0:T(1,128)}, f32[8,1,128]{2,1,0:T(1,128)S(1)}, u32[]{:S(2)}) copy-start(f32[8,1,128]{2,1,0:T(1,128)S(1)} %convert_element_type.151) | copy-start | bytes 12292
  38.7 28.5 %copy-start.25 = (f32[1024]{0:T(1024)}, f32[1024]{0:T(1024)S(1)}, u32[]{:S(2)}) copy-start(f32[1024]{0:T(1024)S(1)} %broadcast_multiply_fusion.1) | copy-start | bytes 12292
  40.0 27.3 copy-start.29
  40.2 46.9 %copy-start.21 = (f32[1024,8]{0,1:T(8,128)}, f32[1024,8]{0,1:T(8,128)S(1)}, u32[]{:S(2)}) copy-start(f32[1024,8]{0,1:T(8,128)S(1)} %get-tuple-element.464) | copy-start | bytes 98308
  40.2 46.9 %copy-start.23 = (f32[1024,8]{0,1:T(8,128)}, f32[1024,8]{0,1:T(8,128)S(1)}, u32[]{:S(2)}) copy-start(f32[1024,8]{0,1:T(8,128)S(1)} %get-tuple-element.465) | copy-start | bytes 98308
  91.3 476.6 %all-gather.16.cloned.1.call-start = ((), (), s32[]{:S(2)}) async-start(), calls=%async_computation.7 | async-start | bytes 10485760 | tf_op jit(solution)/shard_map/all_gather | solution.py:152
  93.9 17.7 copy-start.20
  96.5 638.7 %all-gather.20.cloned.1.call-start = ((), (), s32[]{:S(2)}) async-start(), calls=%async_computation.9 | async-start | bytes 2359296 | tf_op jit(solution)/shard_map/all_gather | solution.py:106
  97.0 1395.9 %all-gather.22.cloned.1.call-start = ((), (), s32[]{:S(2)}) async-start(), calls=%async_computation.10 | async-start | bytes 9437184 | tf_op jit(solution)/shard_map/all_gather | solution.py:110
  97.6 1447.7 %all-gather.24.cloned.1.call-start = ((), (), s32[]{:S(2)}) async-start(), calls=%async_computation.11 | async-start | bytes 9437184 | tf_op jit(solution)/shard_map/all_gather | solution.py:112
  98.2 1509.3 %reduce-scatter.7.cloned.1.call-start = ((), (), s32[]{:S(2)}) async-start(), calls=%async_computation.12 | async-start | bytes 10485760 | tf_op jit(solution)/shard_map/reduce_scatter | solution.py:250
  832.4 9.3 copy-start.1
  877.2 9.3 copy-start.1
  922.1 9.3 copy-start.1
  1458.0 291.5 %reduce-scatter.9.cloned.1.call-start = ((), (), s32[]{:S(2)}) async-start(), calls=%async_computation.13 | async-start | bytes 10485760 | tf_op jit(solution)/shard_map/reduce_scatter | solution.py:253
  1458.0 9.6 copy-start.35
  1458.0 18.4 copy-start.37
  1458.7 29.7 %copy-start.15 = (bf16[1,1024,1024]{2,1,0:T(8,128)(2,1)S(1)}, bf16[1,1024,1024]{2,1,0:T(8,128)(2,1)}, u32[]{:S(2)}) copy-start(bf16[1,1024,1024]{2,1,0:T(8,128)(2,1)} %param.22) | copy-start | bytes 6291460
  1458.7 442.3 %reduce-scatter.13.cloned.1.call-start = ((), (), s32[]{:S(2)}) async-start(), calls=%async_computation.15 | async-start | bytes 4325376 | tf_op jit(solution)/shard_map/reduce_scatter | solution.py:287
  1492.8 774.1 %reduce-scatter.15.cloned.1.call-start = ((), (), s32[]{:S(2)}) async-start(), calls=%async_computation.16 | async-start | bytes 17301504 | tf_op jit(solution)/shard_map/reduce_scatter | solution.py:291
  1584.6 1047.4 %reduce-scatter.17.cloned.1.call-start = ((), (), s32[]{:S(2)}) async-start(), calls=%async_computation.17 | async-start | bytes 17301504 | tf_op jit(solution)/shard_map/reduce_scatter | solution.py:293
  1601.3 1190.5 %reduce-scatter.11.cloned.1.call-start = ((), (), s32[]{:S(2)}) async-start(), calls=%async_computation.14 | async-start | bytes 12976128 | tf_op jit(solution)/shard_map/reduce_scatter | solution.py:285
  1613.3 140.1 %copy-start.22 = (f32[1024,8]{0,1:T(8,128)S(1)}, f32[1024,8]{0,1:T(8,128)}, u32[]{:S(2)}) copy-start(f32[1024,8]{0,1:T(8,128)} %copy-done.21) | copy-start | bytes 98308
  1613.3 140.1 %copy-start.24 = (f32[1024,8]{0,1:T(8,128)S(1)}, f32[1024,8]{0,1:T(8,128)}, u32[]{:S(2)}) copy-start(f32[1024,8]{0,1:T(8,128)} %copy-done.23) | copy-start | bytes 98308
  1780.0 13.1 copy-start.18
  1780.0 13.1 copy-start.39
  1795.5 14.9 copy-start.8
  1810.4 13.5 copy-start.32
  (50 other events, 233.5 us)
Sparse Core Ops, SparseCore 0:
  9.9 48.2 all-gather.13
  91.4 149.9 all-gather.17
  243.6 147.9 all-gather.15
  393.3 26.0 all-gather.19
  421.1 54.3 all-gather.21
  477.3 54.3 all-gather.23
  1458.1 143.7 reduce-scatter.6
  1604.2 145.1 reduce-scatter.8
  1752.3 148.6 reduce-scatter.12
  1903.7 363.2 reduce-scatter.14
  2269.8 362.1 reduce-scatter.16
  2638.5 153.3 reduce-scatter.10
where the time goes:
time: 2810 us; the launch traced here: 2800 us
  waiting for transfers between devices  1170 us (42%)
  matrix products  1110 us (40%)
  other arithmetic  202 us (7%)
  blocking collectives  134 us (5%)
  local copies, waits for them, and re-layouts  129 us (5%)
  loops' own time  34 us (1%)
    reduce_scatter x1, waiting for transfers between devices, local(): lax.psum_scatter(grad_weight_in, ('fsdp', 'ctx'), scatter_dimension=0, ti...  366 us
    reduce_scatter x1, waiting for transfers between devices, local(): lax.psum_scatter(grad_weight_out, ('fsdp', 'ctx'), scatter_dimension=0, t...  365 us
    dot_general x32, matrix products, scores_of(): jnp.einsum('gqhd,gkhd->ghqk', queries, keys_blk, preferred_element_type=j...  299 us
    reduce_scatter x1, waiting for transfers between devices, local(): lax.psum_scatter(grad_weight_qkv, ('fsdp', 'ctx'), scatter_dimension=0, t...  160 us
    dot_general x16, matrix products, back_step(): jnp.einsum('ghqk,gqhd->gkhd', rounded, grad_att, preferred_element_type=f32)  158 us
    reduce_sum x16, other arithmetic, total_step(): jnp.sum(jnp.where(mask, jnp.exp(scores - fresh[..., None]), 0.0), axis=-1)  149 us
    dot_general x16, matrix products, block_grads(): jnp.einsum('gqhd,gkhd->ghqk', grad_att, values_blk, preferred_element_typ...  144 us
    dot_general x16, matrix products, attend_step(): jnp.einsum('ghqk,gkhd->gqhd', probs.astype(bf16), values_blk, preferred_e...  141 us
  transfers between devices with their start and end apart: 12, of which 7 were waited for; matrix products, arithmetic and copies ran while one was open for 48% of the time, Pallas kernels for 0%

commit v1 on v0

--- a/solution.py
+++ b/solution.py
@@ -10,6 +10,22 @@
 ROT = 16
 NORM_EPS = 1e-05
 MASKED = -1e30
+
+
+def collect(x, axis, dim):
+    ways, here, step = (lax.axis_size(axis), lax.axis_index(axis), x.shape[dim])
+    dims = [n * ways if d == dim else n for d, n in enumerate(x.shape)]
+    full = lax.dynamic_update_slice_in_dim(jnp.zeros(dims, x.dtype), x, here * step, axis=dim)
+    going_up = going_down = x
+    for far in range(1, ways // 2 + 1):
+        going_up = lax.ppermute(going_up, axis, [(d, (d + 1) % ways) for d in range(ways)])
+        full = lax.dynamic_update_slice_in_dim(full, going_up, (here - far) % ways * step, axis=dim)
+        if 2 * far < ways:
+            going_down = lax.ppermute(going_down, axis, [(d, (d - 1) % ways) for d in range(ways)])
+            full = lax.dynamic_update_slice_in_dim(
+                full, going_down, (here + far) % ways * step, axis=dim
+            )
+    return full
 
 
 def layer_norm(values, scaling, offset):
@@ -148,7 +164,7 @@
     keys_own = rotate(split_heads(projected[:, width : 2 * width]), cosine, sine).astype(bf16)
     values_own = split_heads(projected[:, 2 * width :]).astype(bf16)
     keys_all, values_all = (
-        lax.all_gather(keys_own, "ctx", axis=1, tiled=True),
+        collect(keys_own, "ctx", 1),
         lax.all_gather(values_own, "ctx", axis=1, tiled=True),
     )
 

time: 2810 us -> 2960 us (1.053)
  starting transfers between devices: 0.48 us -> 86.5 us
  blocking collectives: 134 us -> 196 us
    all_gather x1 -> x0, waiting for transfers between devices: 108 us -> none  [local(): lax.all_gather(keys_own, 'ctx', axis=1, tiled=True)]
    ppermute x0 -> x3, waiting for transfers between devices: none -> 91.7 us  [the longest x2 91.7 us: collect(): lax.ppermute(going_up, axis, [(d, (d + 1) % ways) for d in range(ways)])]
    ppermute x0 -> x3, starting transfers between devices: none -> 86.1 us  [the longest x2 83.7 us: collect(): lax.ppermute(going_up, axis, [(d, (d + 1) % ways) for d in range(ways)])]
    all_gather x1, blocking collectives: 13.3 us -> 79.9 us  [local(): lax.all_gather(positions, 'ctx', axis=1, tiled=True)]
  transfers between devices with their start and end apart: 12 -> 14, of which waited for: 7 -> 7; matrix products, arithmetic and copies ran while one was open for 48% -> 47% of each run, Pallas kernels for 0% -> 0%
where the time goes in v1:
time: 2960 us; the launch traced here: 2950 us
  waiting for transfers between devices  1160 us (39%)
  matrix products  1110 us (38%)
  other arithmetic  203 us (7%)
  blocking collectives  196 us (7%)
  local copies, waits for them, and re-layouts  147 us (5%)
  starting transfers between devices  86.5 us (3%)
  loops' own time  34.3 us (1%)
    reduce_scatter x1, waiting for transfers between devices, local(): lax.psum_scatter(grad_weight_in, ('fsdp', 'ctx'), scatter_dimension=0, ti...  366 us
    reduce_scatter x1, waiting for transfers between devices, local(): lax.psum_scatter(grad_weight_out, ('fsdp', 'ctx'), scatter_dimension=0, t...  365 us
    dot_general x32, matrix products, scores_of(): jnp.einsum('gqhd,gkhd->ghqk', queries, keys_blk, preferred_element_type=j...  297 us
    reduce_scatter x1, waiting for transfers between devices, local(): lax.psum_scatter(grad_weight_qkv, ('fsdp', 'ctx'), scatter_dimension=0, t...  160 us
    dot_general x16, matrix products, back_step(): jnp.einsum('ghqk,gqhd->gkhd', rounded, grad_att, preferred_element_type=f32)  159 us
    reduce_sum x16, other arithmetic, total_step(): jnp.sum(jnp.where(mask, jnp.exp(scores - fresh[..., None]), 0.0), axis=-1)  150 us
    dot_general x16, matrix products, block_grads(): jnp.einsum('gqhd,gkhd->ghqk', grad_att, values_blk, preferred_element_typ...  144 us
    dot_general x16, matrix products, attend_step(): jnp.einsum('ghqk,gkhd->gqhd', probs.astype(bf16), values_blk, preferred_e...  141 us
  transfers between devices with their start and end apart: 14, of which 7 were waited for; matrix products, arithmetic and copies ran while one was open for 47% of the time, Pallas kernels for 0%

profile of v1, /device:TPU:0, one launch (start us, length us, event | category | flops | bytes accessed | tf_op | source)
XLA Modules:
  0.0 2949.2 jit_solution(5807888344387737021)
XLA Ops:
  8.0 10.3 all-gather
  38.9 19.3 all-gather.13.cloned.1.call-done
  111.9 91.7 %collective-permute-done = bf16[1,1024,16,64]{1,3,2,0:T(8,128)(2,1)} collective-permute-done((bf16[1,1024,16,64]{1,3,2,0:T(8,128)(2,1)}, bf16[1,1024,16,64]{1,3,2,0:T(8,128)(2,1)}, u32[]{:S(2)}, u32[]{:S(2)}) %collective-permute-start) | collective-permute-done | bytes 2097184 | tf_op jit(solution)/shard_map/ppermute | solution.py:21
  203.5 82.3 %collective-permute-start.2 = (bf16[1,1024,16,64]{1,3,2,0:T(8,128)(2,1)}, bf16[1,1024,16,64]{1,3,2,0:T(8,128)(2,1)}, u32[]{:S(2)}, u32[]{:S(2)}) collective-permute-start(bf16[1,1024,16,64]{1,3,2,0:T(8,128)(2,1)} %collective-permute-done), channel_id=1, source_target_pairs={{0,1},{1,2},{2,3},{3,0},{4,5},{5,6},{6,7},{7,4},{8,9},{9,10},{10,1... | collective-permute-start | bytes 6291464 | tf_op jit(solution)/shard_map/ppermute | solution.py:21
  286.0 79.9 %all_gather.48 = s32[1,4096]{1,0:T(1,128)S(1)} all-gather(s32[1,1024]{1,0:T(1,128)S(1)} %copy-done.19), channel_id=1, replica_groups=mesh['fsdp'=8,'ctx'=4] {'ctx'}, dimensions={1}, use_global_device_ids=true | all-gather | bytes 20480 | tf_op jit(solution)/shard_map/all_gather | solution.py:134
  365.9 13.1 all_gather.47
  392.7 326.5 %while.39 = (s32[]{:T(128)}, f32[1,16,1024]{2,1,0:T(8,128)S(1)}, f32[1,16,1024]{2,1,0:T(8,128)S(1)}, s32[16]{0:T(128)S(1)}, s32[1,4096]{1,0:T(1,128)S(1)}, /*ind...) while((s32[]{:T(128)}, f32[1,16,1024]{2,1,0:T(8,128)S(1)}, ...), condition=%wide.region_5.6_spmd.clone, body=%wide.region_2.5_spmd.clone.sunk | while | flops 563167488 | bytes 37830352 | solution.py:192
  424.3 10.3 select_reduce_fusion.2
  445.6 10.6 select_reduce_fusion.2
  719.3 167.3 %while.40 = (s32[]{:T(128)}, f32[1,1024,16,64]{1,3,2,0:T(8,128)}, s32[16]{0:T(128)S(1)}, bf16[1,4096,16,64]{1,3,2,0:T(8,128)(2,1)}, s32[1,4096]{1,0:T(1,128)S(1)...) while((s32[]{:T(128)}, f32[1,1024,16,64]{1,3,2,0:T(8,128)}, ...), condition=%wide.region_7.8_spmd.clone, body=%wide.region_6.7_spmd.clone.sunk | while | flops 1089470720 | bytes 12141780 | solution.py:208
  893.8 715.8 %while.41 = (s32[]{:T(128)}, f32[1,1024,16,64]{1,3,2,0:T(8,128)}, bf16[16,1,256,16,64]{2,4,3,1,0:T(8,128)(2,1)}, bf16[16,1,256,16,64]{2,4,3,1,0:T(8,128)(2,1)}, ...) while((s32[]{:T(128)}, f32[1,1024,16,64]{1,3,2,0:T(8,128)}, ...), condition=%wide.region_9.10_spmd.clone, body=%wide.region_8.9_spmd.clone.sunk | while | flops 2721054976 | bytes 138887984 | solution.py:262
  927.5 10.0 fusion.176
  1062.0 9.9 fusion.176
  1286.0 9.9 fusion.176
  1375.5 9.9 fusion.176
  1420.4 9.9 fusion.176
  1465.2 9.9 fusion.176
  1510.0 9.9 fusion.176
  1646.1 51.1 %multiply_convert_fusion = (bf16[1024,4096]{1,0:T(8,128)(2,1)}, f32[1024,4096]{1,0:T(8,128)}, f32[1024,4096]{1,0:T(8,128)}) fusion(f32[4096]{0:T(1024)S(1)} %bitcast.419, bf16[1024,4096]{1,0:T(8,128)(2,1)} %all-gather.19.cloned.1.call-done, bf16[1,1024,1024]{2,1,0:T(8,128)(2,1)S(1)} %copy-done.3, f32[1024]{0:T(1024)S(1)} %bitcast.424, ...), kind=kOutput, calls=%fused_computation.67 | convolution fusion | flops 8873050112 | bytes 52461568 | tf_op jit(solution)/shard_map/dot_general | solution.py:210
  1697.2 24.2 convert_reduce_fusion
  1721.4 15.2 fusion.109
  1736.7 16.6 fusion.95
  1765.0 135.0 %reduce-scatter.9.cloned.1.call-done = bf16[4,1,256,16,64]{2,4,3,1,0:T(8,128)(2,1)} async-done(((bf16[16,1,256,16,64]{2,4,3,1,0:T(8,128)(2,1)}), bf16[4,1,256,16,64]{2,4,3,1,0:T(8,128)(2,1)}) %reduce-scatter.9.cloned.1.call-update) | async-done | bytes 2097168 | tf_op jit(solution)/shard_map/reduce_scatter | solution.py:269
  1909.5 11.7 fusion.113
  1930.6 13.1 fusion.124
  1946.1 14.9 fusion.94
  1961.0 13.5 fusion.120
  1989.1 41.5 %all-reduce.7 = (f32[1024]{0:T(1024)S(1)}, f32[1024]{0:T(1024)S(1)}, f32[3072]{0:T(1024)S(1)}, f32[1024]{0:T(1024)S(1)}, f32[1024]{0:T(1024)S(1)}, /*index=5*/f32[1024]{0:T(1024)S(1)}, f32[4096]{0:T(1024)S(1)}) all-reduce(f32[1024]{0:T(1024)S(1)} %get-tuple-element.356, ...), channel_id=4, replica_groups=mesh['fsdp'=8,'ctx'=4] {'fsdp','ctx'}, use_global_device_ids=true, to_apply=%region_17.18.clone | all-reduce | flops 12288 | bytes 98304
  2034.7 17.0 reduce-scatter.13.cloned.1.call-done
  2051.7 365.7 %reduce-scatter.15.cloned.1.call-done = f32[32,4096]{1,0:T(8,128)} async-done(((f32[1024,4096]{1,0:T(8,128)}), f32[32,4096]{1,0:T(8,128)}) %reduce-scatter.15.cloned.1.call-update) | async-done | bytes 524304 | tf_op jit(solution)/shard_map/reduce_scatter | solution.py:307
  2417.4 364.9 %reduce-scatter.17.cloned.1.call-done = f32[128,1024]{1,0:T(8,128)} async-done(((f32[4096,1024]{1,0:T(8,128)}), f32[128,1024]{1,0:T(8,128)}) %reduce-scatter.17.cloned.1.call-update) | async-done | bytes 524304 | tf_op jit(solution)/shard_map/reduce_scatter | solution.py:309
  2782.3 160.0 %reduce-scatter.11.cloned.1.call-done = f32[32,3072]{1,0:T(8,128)} async-done(((f32[1024,3072]{1,0:T(8,128)}), f32[32,3072]{1,0:T(8,128)}) %reduce-scatter.11.cloned.1.call-update) | async-done | bytes 393232 | tf_op jit(solution)/shard_map/reduce_scatter | solution.py:301
  (603 shorter events, 1268.6 us)
Async XLA Ops:
  7.2 30.4 %copy-start.2 = (bf16[1,1024,1024]{2,1,0:T(8,128)(2,1)S(1)}, bf16[1,1024,1024]{2,1,0:T(8,128)(2,1)}, u32[]{:S(2)}) copy-start(bf16[1,1024,1024]{2,1,0:T(8,128)(2,1)} %param.21) | copy-start | bytes 6291460
  7.2 51.0 %all-gather.13.cloned.1.call-start = ((), (), s32[]{:S(2)}) async-start(), calls=%async_computation.6 | async-start | bytes 7077888 | tf_op jit(solution)/shard_map/all_gather | solution.py:120
  7.9 711.3 %all-gather.15.cloned.1.call-start = ((), (), s32[]{:S(2)}) async-start(), calls=%async_computation.7 | async-start | bytes 10485760 | tf_op jit(solution)/shard_map/all_gather | solution.py:168
  18.3 48.9 %copy-start.27 = (f32[8,1,128]{2,1,0:T(1,128)}, f32[8,1,128]{2,1,0:T(1,128)S(1)}, u32[]{:S(2)}) copy-start(f32[8,1,128]{2,1,0:T(1,128)S(1)} %convert_element_type.150) | copy-start | bytes 12292
  26.9 40.3 %copy-start.33 = (f32[8,1,128]{2,1,0:T(1,128)}, f32[8,1,128]{2,1,0:T(1,128)S(1)}, u32[]{:S(2)}) copy-start(f32[8,1,128]{2,1,0:T(1,128)S(1)} %convert_element_type.151) | copy-start | bytes 12292
  37.6 29.6 %copy-start.25 = (f32[1024]{0:T(1024)}, f32[1024]{0:T(1024)S(1)}, u32[]{:S(2)}) copy-start(f32[1024]{0:T(1024)S(1)} %broadcast_multiply_fusion.1) | copy-start | bytes 12292
  38.9 28.3 copy-start.29
  74.7 811.9 %all-gather.17.cloned.1.call-start = ((), (), s32[]{:S(2)}) async-start(), calls=%async_computation.8 | async-start | bytes 2359296 | tf_op jit(solution)/shard_map/all_gather | solution.py:122
  75.4 1569.2 %all-gather.19.cloned.1.call-start = ((), (), s32[]{:S(2)}) async-start(), calls=%async_computation.9 | async-start | bytes 9437184 | tf_op jit(solution)/shard_map/all_gather | solution.py:126
  76.0 1621.2 %all-gather.21.cloned.1.call-start = ((), (), s32[]{:S(2)}) async-start(), calls=%async_computation.10 | async-start | bytes 9437184 | tf_op jit(solution)/shard_map/all_gather | solution.py:128
  76.3 22.0 copy-start.21
  76.3 22.0 copy-start.23
  105.2 260.7 %copy-start.20 = (s32[1,1024]{1,0:T(1,128)S(1)}, s32[1,1024]{1,0:T(1,128)}, u32[]{:S(2)}) copy-start(s32[1,1024]{1,0:T(1,128)} %param.24) | copy-start | bytes 12292
  108.0 95.5 %collective-permute-start = (bf16[1,1024,16,64]{1,3,2,0:T(8,128)(2,1)}, bf16[1,1024,16,64]{1,3,2,0:T(8,128)(2,1)}, u32[]{:S(2)}, u32[]{:S(2)}) collective-permute-start(bf16[1,1024,16,64]{1,3,2,0:T(8,128)(2,1)} %get-tuple-element.460), channel_id=1, source_target_pairs={{0,1},{1,2},{2,3},{3,0},{4,5},{5,6},{6,7},{7,4},{8,9},{9,10},{10,1... | collective-permute-start | bytes 6291464 | tf_op jit(solution)/shard_map/ppermute | solution.py:21
  109.4 276.9 %collective-permute-start.1 = (bf16[1,1024,16,64]{1,3,2,0:T(8,128)(2,1)}, bf16[1,1024,16,64]{1,3,2,0:T(8,128)(2,1)}, u32[]{:S(2)}, u32[]{:S(2)}) collective-permute-start(bf16[1,1024,16,64]{1,3,2,0:T(8,128)(2,1)} %get-tuple-element.460), channel_id=1, source_target_pairs={{0,3},{1,0},{2,1},{3,2},{4,7},{5,4},{6,5},{7,6},{8,11},{9,8},{10,9... | collective-permute-start | bytes 6291464 | tf_op jit(solution)/shard_map/ppermute | solution.py:24
  203.5 186.0 %collective-permute-start.2 = (bf16[1,1024,16,64]{1,3,2,0:T(8,128)(2,1)}, bf16[1,1024,16,64]{1,3,2,0:T(8,128)(2,1)}, u32[]{:S(2)}, u32[]{:S(2)}) collective-permute-start(bf16[1,1024,16,64]{1,3,2,0:T(8,128)(2,1)} %collective-permute-done), channel_id=1, source_target_pairs={{0,1},{1,2},{2,3},{3,0},{4,5},{5,6},{6,7},{7,4},{8,9},{9,10},{10,1... | collective-permute-start | bytes 6291464 | tf_op jit(solution)/shard_map/ppermute | solution.py:21
  285.8 1473.5 %reduce-scatter.7.cloned.1.call-start = ((), (), s32[]{:S(2)}) async-start(), calls=%async_computation.11 | async-start | bytes 10485760 | tf_op jit(solution)/shard_map/reduce_scatter | solution.py:266
  1566.3 9.3 copy-start.1
  1609.6 290.5 %reduce-scatter.9.cloned.1.call-start = ((), (), s32[]{:S(2)}) async-start(), calls=%async_computation.12 | async-start | bytes 10485760 | tf_op jit(solution)/shard_map/reduce_scatter | solution.py:269
  1609.6 9.8 copy-start.35
  1609.6 18.6 copy-start.37
  1610.3 29.8 %copy-start.15 = (bf16[1,1024,1024]{2,1,0:T(8,128)(2,1)S(1)}, bf16[1,1024,1024]{2,1,0:T(8,128)(2,1)}, u32[]{:S(2)}) copy-start(bf16[1,1024,1024]{2,1,0:T(8,128)(2,1)} %param.22) | copy-start | bytes 6291460
  1610.3 441.4 %reduce-scatter.13.cloned.1.call-start = ((), (), s32[]{:S(2)}) async-start(), calls=%async_computation.14 | async-start | bytes 4325376 | tf_op jit(solution)/shard_map/reduce_scatter | solution.py:303
  1644.6 772.8 %reduce-scatter.15.cloned.1.call-start = ((), (), s32[]{:S(2)}) async-start(), calls=%async_computation.15 | async-start | bytes 17301504 | tf_op jit(solution)/shard_map/reduce_scatter | solution.py:307
  1736.6 1045.7 %reduce-scatter.17.cloned.1.call-start = ((), (), s32[]{:S(2)}) async-start(), calls=%async_computation.16 | async-start | bytes 17301504 | tf_op jit(solution)/shard_map/reduce_scatter | solution.py:309
  1753.3 1189.0 %reduce-scatter.11.cloned.1.call-start = ((), (), s32[]{:S(2)}) async-start(), calls=%async_computation.13 | async-start | bytes 12976128 | tf_op jit(solution)/shard_map/reduce_scatter | solution.py:301
  1765.0 138.9 %copy-start.22 = (f32[1024,8]{0,1:T(8,128)S(1)}, f32[1024,8]{0,1:T(8,128)}, u32[]{:S(2)}) copy-start(f32[1024,8]{0,1:T(8,128)} %copy-done.21) | copy-start | bytes 98308
  1765.0 138.9 %copy-start.24 = (f32[1024,8]{0,1:T(8,128)S(1)}, f32[1024,8]{0,1:T(8,128)}, u32[]{:S(2)}) copy-start(f32[1024,8]{0,1:T(8,128)} %copy-done.23) | copy-start | bytes 98308
  1930.6 13.1 copy-start.18
  1930.6 13.1 copy-start.39
  1946.1 14.9 copy-start.8
  1961.0 13.5 copy-start.32
  (52 other events, 249.2 us)
Sparse Core Ops, SparseCore 0:
  9.9 48.2 all-gather.12
  74.8 257.7 all-gather.14
  334.5 26.9 all-gather.16
  363.2 54.3 all-gather.18
  419.4 54.3 all-gather.20
  1609.7 142.7 reduce-scatter.6
  1754.8 145.1 reduce-scatter.8
  1902.9 148.7 reduce-scatter.12
  2054.6 362.7 reduce-scatter.14
  2420.1 362.1 reduce-scatter.16
  2788.9 153.3 reduce-scatter.10
